TPU v7x, 128 devices: a whole 4x4x4 slice. The times are simulated.
128 devices in a mesh: dp: 8 (over z, core), mp: 16 (over y, x).
Axes of the slice: x: 4, y: 4, z: 4, core: 2. Of those that a mesh axis runs over, the one named last changes fastest.
Arguments:
- acts: bfloat16 [1024, 8192], P('dp', 'mp'), may hold values from -6 to 6
- w_up: bfloat16 [8192, 14336], P(None, 'mp'), may hold values from -0.0625 to 0.0625
- out_grad: bfloat16 [1024, 14336], P('dp', 'mp'), may hold values from -6 to 6
- rotation: float32 [8192, 8192], P('mp', 'dp'), may hold values from -6 to 6
Outputs:
- half_rotation: float32 [8192, 8192], P('mp', 'dp')
- next_rotation: float32 [8192, 8192], P('mp', 'dp')
All inputs are finite; a program needn't handle non-finite values.
Results may differ from a plain program's by a relative error of at most 0.017.
Values may be sent and summed in bfloat16 or wider, within the bound.
A program may use at most 128 MiB of HBM per device.

v0:
```python
import functools
import math
import jax
import jax.numpy as jnp
from jax import lax
from jax.sharding import Mesh
from jax.sharding import PartitionSpec as P

D = 8192
ITERS = 2
DP = ("dp_0", "dp_1")
MP = ("mp_0", "mp_1")
DP_MP = ("dp_0", "dp_1", "mp_0", "mp_1")
step_gain = 0.5
epsilon = 1e-06


def by_axis(value, axes):
    return functools.reduce(lax.psum, axes, value)


def in_one_piece(arrays, axis, dim, along):
    both = jnp.concatenate(arrays, axis=along)
    filled, at, gathered = (lax.all_gather(both, axis, axis=dim, tiled=True), 0, [])
    for a in arrays:
        gathered.append(lax.slice_in_dim(filled, at, at + a.shape[along], axis=along))
        at += a.shape[along]
    return tuple(gathered)


def settle(term):
    return lax.optimization_barrier(term.astype(jnp.bfloat16)).astype(jnp.float32)


def contract_cols(left, right):
    return lax.dot_general(
        left, right, (((1,), (1,)), ((), ())), preferred_element_type=jnp.float32
    )


def local(acts, w_up, out_grad, rotation):
    inv_root = D ** (-0.5)
    rot_half = rotation.astype(jnp.bfloat16)
    rot_rows = lax.all_gather(rot_half, DP, axis=1, tiled=True)
    mixed = lax.psum(
        (jnp.dot(acts, rot_rows, preferred_element_type=jnp.float32) * inv_root).astype(
            jnp.bfloat16
        ),
        MP,
    )
    hidden = jnp.dot(mixed, w_up, preferred_element_type=jnp.float32)
    sigmoid_hidden = jax.nn.sigmoid(hidden)
    grad_hidden = (
        out_grad.astype(jnp.float32) * sigmoid_hidden * (1.0 + hidden * (1.0 - sigmoid_hidden))
    ).astype(jnp.bfloat16)
    grad_mixed = lax.psum(contract_cols(grad_hidden, w_up).astype(jnp.bfloat16), MP)
    factor = contract_cols(grad_mixed, rot_rows).astype(jnp.bfloat16)
    act_norm, factor_norm = (
        by_axis(jnp.sum(jnp.square(acts.astype(jnp.float32))), DP_MP),
        by_axis(jnp.sum(jnp.square(factor.astype(jnp.float32))), DP_MP),
    )
    token_count = acts.shape[0] * lax.axis_size(DP)
    spread = (token_count ** (-0.5) + D ** (-0.5)) ** 2
    step_size = (
        step_gain
        * math.sqrt(D)
        / (jnp.sqrt((act_norm + epsilon) * (factor_norm + epsilon)) * spread)
    )
    every_acts, every_factor = in_one_piece((acts, factor), DP, 0, 1)
    groups = lax.axis_size(DP)
    block_rows = acts.shape[0]
    acts_blocks = every_acts.reshape(groups, block_rows, -1)
    factor_blocks = every_factor.reshape(groups, block_rows, -1)
    current = rotation
    first_iterate = rotation
    for iteration in range(ITERS):
        point = (rotation + current).astype(jnp.bfloat16)
        left_sum, right_sum = (
            lax.psum(
                (
                    jnp.dot(every_factor, point, preferred_element_type=jnp.float32) * inv_root
                ).astype(jnp.bfloat16),
                MP,
            ).astype(jnp.float32),
            lax.psum(
                (jnp.dot(every_acts, point, preferred_element_type=jnp.float32) * inv_root).astype(
                    jnp.bfloat16
                ),
                MP,
            ).astype(jnp.float32),
        )
        left = left_sum.astype(jnp.bfloat16).reshape(groups, block_rows, -1)
        right = right_sum.astype(jnp.bfloat16).reshape(groups, block_rows, -1)
        terms = jnp.einsum(
            "ntr,ntc->nrc", acts_blocks, left, preferred_element_type=jnp.float32
        ) - jnp.einsum("ntr,ntc->nrc", factor_blocks, right, preferred_element_type=jnp.float32)
        update = jnp.sum(settle(terms), axis=0)
        current = rotation - step_size * update
        if iteration == 0:
            first_iterate = current
    return (first_iterate, current)


def solution(mesh):
    finer = Mesh(mesh.devices.reshape(4, 2, 4, 4), ("dp_0", "dp_1", "mp_0", "mp_1"))
    placed = (P(DP, MP), P(None, MP), P(DP, MP), P(MP, DP))
    return jax.shard_map(
        local, mesh=finer, in_specs=placed, out_specs=(P(MP, DP), P(MP, DP)), check_vma=False
    )
```

profile of v0, /device:TPU:1, one launch (start us, length us, event | category | flops | bytes accessed | tf_op | source)
XLA Modules:
  0.0 586.6 jit_solution(2937792211861183039)
XLA Ops:
  7.2 0.0 copy-start.7
  7.2 0.0 all-gather.3.cloned.1.call-start
  7.2 2.8 convert_element_type.64
  10.0 0.0 all-gather.3.cloned.1.call-update
  10.0 0.0 all-reduce.11.cloned.1.call-start
  10.0 53.8 %all-gather.3.cloned.1.call-done = bf16[512,8192]{1,0:T(8,128)(2,1)} async-done(((bf16[512,1024]{1,0:T(8,128)(2,1)}), bf16[512,8192]{1,0:T(8,128)(2,1)}) %all-gather.3.cloned.1.call-update) | async-done | bytes 8388624 | tf_op jit(solution)/shard_map/all_gather | solution.py:44
  63.8 0.0 copy-done.7
  63.8 6.0 %fusion = bf16[128,8192]{1,0:T(8,128)(2,1)} fusion(bf16[128,512]{1,0:T(8,128)(2,1)S(1)} %copy-done.7, bf16[512,8192]{1,0:T(8,128)(2,1)} %all-gather.3.cloned.1.call-done), kind=kOutput, calls=%fused_computation.5 | convolution fusion | flops 1075838976 | bytes 10616832 | tf_op jit(solution)/shard_map/dot_general | solution.py:46
  69.9 0.0 copy-start.8
  69.9 0.0 all-reduce.11.cloned.1.call-update
  69.9 0.0 all-reduce.13.cloned.1.call-start
  69.9 88.7 %all-reduce.11.cloned.1.call-done = bf16[128,8192]{1,0:T(8,128)(2,1)} async-done(((bf16[128,8192]{1,0:T(8,128)(2,1)}), bf16[128,8192]{1,0:T(8,128)(2,1)}) %all-reduce.11.cloned.1.call-update) | async-done | bytes 2097168 | tf_op jit(solution)/shard_map/psum | solution.py:45
  158.6 0.0 copy-done.8
  158.6 20.2 %convolution_convert_fusion = bf16[128,8192]{1,0:T(8,128)(2,1)} fusion(bf16[8192,896]{1,0:T(8,128)(2,1)} %param.5, bf16[128,896]{1,0:T(8,128)(2,1)S(1)} %copy-done.8, bf16[128,8192]{1,0:T(8,128)(2,1)} %all-reduce.11.cloned.1.call-done), kind=kOutput, calls=%fused_computation.6 | convolution fusion | flops 3760291840 | bytes 19103744 | tf_op jit(solution)/shard_map/dot_general | solution.py:36
  178.8 0.0 all-reduce.13.cloned.1.call-update
  178.8 0.0 copy-start
  178.8 0.0 all-gather.5.cloned.1.call-start
  178.9 89.5 %all-reduce.13.cloned.1.call-done = bf16[128,8192]{1,0:T(8,128)(2,1)} async-done(((bf16[128,8192]{1,0:T(8,128)(2,1)}), bf16[128,8192]{1,0:T(8,128)(2,1)}) %all-reduce.13.cloned.1.call-update) | async-done | bytes 2097168 | tf_op jit(solution)/shard_map/psum | solution.py:56
  268.4 7.7 %multiply_reduce_fusion = (f32[]{:T(128)}, bf16[128,512]{1,0:T(8,128)(2,1)S(1)}) fusion(bf16[128,8192]{1,0:T(8,128)(2,1)} %all-reduce.13.cloned.1.call-done, bf16[512,8192]{1,0:T(8,128)(2,1)} %all-gather.3.cloned.1.call-done), kind=kOutput, calls=%fused_computation.18 | convolution fusion | flops 1074003968 | bytes 10616836 | tf_op jit(solution)/shard_map/dot_general | solution.py:36
  276.1 0.7 pad_maximum_fusion
  276.8 0.0 all-gather.5.cloned.1.call-update
  276.8 0.0 all-reduce.17.cloned.1.call-start
  276.9 26.4 %all-gather.5.cloned.1.call-done = bf16[1024,1024]{1,0:T(8,128)(2,1)} async-done(((bf16[128,1024]{1,0:T(8,128)(2,1)}), bf16[1024,1024]{1,0:T(8,128)(2,1)}) %all-gather.5.cloned.1.call-update) | async-done | bytes 2097168 | tf_op jit(solution)/shard_map/all_gather | solution.py:24
  303.3 0.0 copy-done
  303.3 0.0 copy-start.5
  303.3 4.0 multiply_convert_fusion.3
  307.2 0.0 copy-done.5
  307.2 2.6 multiply_convert_fusion.2
  309.8 0.0 all-reduce.17.cloned.1.call-update
  309.8 0.0 all-reduce.15.cloned.1.call-start
  309.9 0.7 multiply_reduce_fusion.1
  310.6 7.9 %all-reduce.2 = (f32[]{:T(128)}, f32[]{:T(128)}) all-reduce(f32[]{:T(128)} %multiply_reduce_fusion.1, f32[]{:T(128)} %get-tuple-element.18), channel_id=1, replica_groups=mesh['dp_0'=4,'dp_1'=2,'mp_0'=4,'mp_1'=4] {'dp_0'}, use_global_device_ids=true, to_apply=%region_1.0 | all-reduce | flops 2 | bytes 16 | tf_op jit(solution)/shard_map/psum | solution.py:19
  318.5 5.1 all-reduce.3
  323.6 9.9 %all-reduce.1 = (f32[]{:T(128)}, f32[]{:T(128)}) all-reduce(f32[]{:T(128)} %get-tuple-element.8, f32[]{:T(128)} %get-tuple-element.9), channel_id=1, replica_groups=mesh['dp_0'=4,'dp_1'=2,'mp_0'=4,'mp_1'=4] {'mp_0'}, use_global_device_ids=true, to_apply=%region_3.0 | all-reduce | flops 2 | bytes 16 | tf_op jit(solution)/shard_map/psum | solution.py:19
  333.5 9.3 %all-reduce = (f32[]{:T(128)}, f32[]{:T(128)}) all-reduce(f32[]{:T(128)} %get-tuple-element.4, f32[]{:T(128)} %get-tuple-element.5), channel_id=1, replica_groups=mesh['dp_0'=4,'dp_1'=2,'mp_0'=4,'mp_1'=4] {'mp_1'}, use_global_device_ids=true, to_apply=%region_4.0 | all-reduce | flops 2 | bytes 16 | tf_op jit(solution)/shard_map/psum | solution.py:19
  344.2 2.6 fusion.7
  346.9 66.5 %all-reduce.17.cloned.1.call-done = (bf16[8,128,1024]{2,1,0:T(8,128)(2,1)}, bf16[8,128,1024]{2,1,0:T(8,128)(2,1)}) async-done(((bf16[8,128,1024]{2,1,0:T(8,128)(2,1)}, bf16[8,128,1024]{2,1,0:T(8,128)(2,1)}), (bf16[8,128,1024]{2,1,0:T(8,128)(2,1)}, bf16[8,128,1024]{2,1,0:T(8,128)(2,1)})) %all-reduce.17.cloned.1.call-update) | async-done | bytes 4194320 | tf_op jit(solution)/shard_map/psum | solution.py:79
  413.4 0.0 copy-start.1
  413.4 0.0 copy-start.3
  413.4 9.8 %fusion.10 = f32[8,512,1024]{2,1,0:T(8,128)} fusion(bf16[8,128,512]{2,1,0:T(8,128)(2,1)S(1)} %bitcast.23, bf16[8,128,1024]{2,1,0:T(8,128)(2,1)} %get-tuple-element.12), kind=kOutput, calls=%fused_computation.28 | convolution fusion | flops 1073741824 | bytes 19922944 | tf_op jit(solution)/shard_map/ntr,ntc->nrc/dot_general | solution.py:94
  423.2 0.0 copy-done.1
  423.2 0.0 copy-done.3
  423.2 11.4 %subtract_convert_fusion.1 = bf16[8,512,1024]{2,1,0:T(8,128)(2,1)} fusion(f32[8,512,1024]{2,1,0:T(8,128)} %fusion.10, bf16[8,128,512]{2,1,0:T(8,128)(2,1)S(1)} %bitcast.25, bf16[8,128,1024]{2,1,0:T(8,128)(2,1)S(1)} %copy-done.3), kind=kOutput, calls=%fused_computation.3 | convolution fusion | flops 1082130432 | bytes 28311552 | tf_op jit(solution)/shard_map/ntr,ntc->nrc/dot_general | solution.py:96
  434.6 5.7 convert_reduce_fusion.1
  440.3 0.0 copy-start.6
  440.3 1.8 add_convert_fusion
  442.2 0.0 copy-done.6
  442.2 2.6 multiply_convert_fusion
  444.8 2.6 multiply_convert_fusion.1
  447.4 0.0 all-reduce.15.cloned.1.call-update
  447.4 103.4 %all-reduce.15.cloned.1.call-done = (bf16[8,128,1024]{2,1,0:T(8,128)(2,1)}, bf16[8,128,1024]{2,1,0:T(8,128)(2,1)}) async-done(((bf16[8,128,1024]{2,1,0:T(8,128)(2,1)}, bf16[8,128,1024]{2,1,0:T(8,128)(2,1)}), (bf16[8,128,1024]{2,1,0:T(8,128)(2,1)}, bf16[8,128,1024]{2,1,0:T(8,128)(2,1)})) %all-reduce.15.cloned.1.call-update) | async-done | bytes 4194320 | tf_op jit(solution)/shard_map/psum | solution.py:79
  550.8 0.0 copy-start.2
  550.8 0.0 copy-start.4
  550.8 9.8 %fusion.11 = f32[8,512,1024]{2,1,0:T(8,128)} fusion(bf16[8,128,512]{2,1,0:T(8,128)(2,1)S(1)} %bitcast.24, bf16[8,128,1024]{2,1,0:T(8,128)(2,1)} %get-tuple-element.10), kind=kOutput, calls=%fused_computation.29 | convolution fusion | flops 1073741824 | bytes 19922944 | tf_op jit(solution)/shard_map/ntr,ntc->nrc/dot_general | solution.py:94
  560.6 0.0 copy-done.2
  560.7 0.0 copy-done.4
  560.7 11.7 %subtract_convert_fusion = bf16[8,512,1024]{2,1,0:T(8,128)(2,1)} fusion(f32[8,512,1024]{2,1,0:T(8,128)} %fusion.11, bf16[8,128,512]{2,1,0:T(8,128)(2,1)S(1)} %bitcast.26, bf16[8,128,1024]{2,1,0:T(8,128)(2,1)S(1)} %copy-done.4), kind=kOutput, calls=%fused_computation.1 | convolution fusion | flops 1082130432 | bytes 28311552 | tf_op jit(solution)/shard_map/ntr,ntc->nrc/dot_general | solution.py:96
  572.3 5.7 convert_reduce_fusion
  578.0 1.8 multiply_subtract_fusion
Async XLA Ops:
  7.2 56.7 %copy-start.7 = (bf16[128,512]{1,0:T(8,128)(2,1)S(1)}, bf16[128,512]{1,0:T(8,128)(2,1)}, u32[]{:S(2)}) copy-start(bf16[128,512]{1,0:T(8,128)(2,1)} %param.4) | copy-start | bytes 393220
  7.2 56.7 %all-gather.3.cloned.1.call-start = ((), (), s32[]{:S(2)}) async-start(), calls=%async_computation | async-start | bytes 9437184 | tf_op jit(solution)/shard_map/all_gather | solution.py:44
  10.0 148.6 %all-reduce.11.cloned.1.call-start = ((), (), s32[]{:S(2)}) async-start(), calls=%async_computation.1 | async-start | bytes 4194304 | tf_op jit(solution)/shard_map/psum | solution.py:45
  69.9 88.8 %copy-start.8 = (bf16[128,896]{1,0:T(8,128)(2,1)S(1)}, bf16[128,896]{1,0:T(8,128)(2,1)}, u32[]{:S(2)}) copy-start(bf16[128,896]{1,0:T(8,128)(2,1)} %param.6) | copy-start | bytes 688132
  69.9 198.5 %all-reduce.13.cloned.1.call-start = ((), (), s32[]{:S(2)}) async-start(), calls=%async_computation.2 | async-start | bytes 4194304 | tf_op jit(solution)/shard_map/psum | solution.py:56
  178.8 124.4 %copy-start = (f32[512,1024]{1,0:T(8,128)S(1)}, f32[512,1024]{1,0:T(8,128)}, u32[]{:S(2)}) copy-start(f32[512,1024]{1,0:T(8,128)} %param.7) | copy-start | bytes 6291460
  178.8 124.4 %all-gather.5.cloned.1.call-start = ((), (), s32[]{:S(2)}) async-start(), calls=%async_computation.3 | async-start | bytes 2359296 | tf_op jit(solution)/shard_map/all_gather | solution.py:24
  276.8 136.5 %all-reduce.17.cloned.1.call-start = ((), (), s32[]{:S(2)}) async-start(), calls=%async_computation.5 | async-start | bytes 8388608 | tf_op jit(solution)/shard_map/psum | solution.py:79
  303.3 4.0 copy-start.5
  309.8 241.0 %all-reduce.15.cloned.1.call-start = ((), (), s32[]{:S(2)}) async-start(), calls=%async_computation.4 | async-start | bytes 8388608 | tf_op jit(solution)/shard_map/psum | solution.py:79
  413.4 9.8 %copy-start.1 = (bf16[1024,512]{1,0:T(8,128)(2,1)S(1)}, bf16[1024,512]{1,0:T(8,128)(2,1)}, u32[]{:S(2)}) copy-start(bf16[1024,512]{1,0:T(8,128)(2,1)} %get-tuple-element.16) | copy-start | bytes 3145732
  413.4 9.8 %copy-start.3 = (bf16[8,128,1024]{2,1,0:T(8,128)(2,1)S(1)}, bf16[8,128,1024]{2,1,0:T(8,128)(2,1)}, u32[]{:S(2)}) copy-start(bf16[8,128,1024]{2,1,0:T(8,128)(2,1)} %get-tuple-element.13) | copy-start | bytes 6291460
  440.3 1.9 copy-start.6
  550.8 9.8 %copy-start.2 = (bf16[1024,512]{1,0:T(8,128)(2,1)S(1)}, bf16[1024,512]{1,0:T(8,128)(2,1)}, u32[]{:S(2)}) copy-start(bf16[1024,512]{1,0:T(8,128)(2,1)} %get-tuple-element.16) | copy-start | bytes 3145732
  550.8 9.8 %copy-start.4 = (bf16[8,128,1024]{2,1,0:T(8,128)(2,1)S(1)}, bf16[8,128,1024]{2,1,0:T(8,128)(2,1)}, u32[]{:S(2)}) copy-start(bf16[8,128,1024]{2,1,0:T(8,128)(2,1)} %get-tuple-element.11) | copy-start | bytes 6291460
Sparse Core Ops, SparseCore 0:
  10.3 53.5 all-gather.2
  70.0 88.5 all-reduce.10
  178.9 89.4 all-reduce.12
  276.9 26.2 all-gather.4
  310.0 103.3 all-reduce.16
  447.5 103.2 all-reduce.14
where the time goes:
time: 587 us
  waiting for transfers between devices  428 us (73%)
  matrix products  88.4 us (15%)
  blocking collectives  32.2 us (5%)
  other arithmetic  19.1 us (3%)
  between operations  15.6 us (3%)
    psum x2, waiting for transfers between devices, local(): lax.psum((jnp.dot(every_factor, point, preferred_element_type=jnp.float32...  170 us
    psum x1, waiting for transfers between devices, local(): lax.psum(contract_cols(grad_hidden, w_up).astype(jnp.bfloat16), MP)  89.5 us
    psum x1, waiting for transfers between devices, local(): lax.psum((jnp.dot(acts, rot_rows, preferred_element_type=jnp.float32) * i...  88.7 us
    all_gather x1, waiting for transfers between devices, local(): rot_rows = lax.all_gather(rot_half, DP, axis=1, tiled=True)  53.8 us
    psum x4, blocking collectives, by_axis(): return functools.reduce(lax.psum, axes, value)  32.2 us
    dot_general x2, matrix products, contract_cols(): lax.dot_general(left, right, (((1,), (1,)), ((), ())), preferred_element_...  27.8 us
    all_gather x1, waiting for transfers between devices, in_one_piece(): lax.all_gather(both, axis, axis=dim, tiled=True)  26.4 us
    dot_general x2, matrix products, local(): jnp.einsum('ntr,ntc->nrc', factor_blocks, right, preferred_element_type=j...  23.1 us
  transfers between devices with their start and end apart: 6, of which 6 were waited for; matrix products, arithmetic and copies ran while one was open for 1% of the time, Pallas kernels for 0%

commit v1 on v0

--- a/solution.py
+++ b/solution.py
@@ -42,11 +42,14 @@
     inv_root = D ** (-0.5)
     rot_half = rotation.astype(jnp.bfloat16)
     rot_rows = lax.all_gather(rot_half, DP, axis=1, tiled=True)
-    mixed = lax.psum(
-        (jnp.dot(acts, rot_rows, preferred_element_type=jnp.float32) * inv_root).astype(
-            jnp.bfloat16
+    mixed = jnp.sum(
+        lax.all_gather(
+            (jnp.dot(acts, rot_rows, preferred_element_type=jnp.float32) * inv_root).astype(
+                jnp.bfloat16
+            ),
+            MP,
         ),
-        MP,
+        axis=0,
     )
     hidden = jnp.dot(mixed, w_up, preferred_element_type=jnp.float32)
     sigmoid_hidden = jax.nn.sigmoid(hidden)

time: 587 us -> 705 us (1.20)
  waiting for transfers between devices: 428 us -> 536 us
  other arithmetic: 19.1 us -> 30.7 us
    all_gather x0 -> x1, waiting for transfers between devices: none -> 197 us  [local(): lax.all_gather((jnp.dot(acts, rot_rows, preferred_element_type=jnp.float3...]
    psum x1 -> x0, waiting for transfers between devices: 88.7 us -> none  [local(): lax.psum((jnp.dot(acts, rot_rows, preferred_element_type=jnp.float32) * i...]
    reduce_sum x0 -> x1, other arithmetic: none -> 11.6 us  [local(): jnp.sum(lax.all_gather((jnp.dot(acts, rot_rows, preferred_element_type=jn...]
  transfers between devices with their start and end apart: 6 -> 6, of which waited for: 6 -> 6; matrix products, arithmetic and copies ran while one was open for 1% -> 0% of each run, Pallas kernels for 0% -> 0%
where the time goes in v1:
time: 705 us
  waiting for transfers between devices  536 us (76%)
  matrix products  87.8 us (12%)
  blocking collectives  32.2 us (5%)
  other arithmetic  30.7 us (4%)
  between operations  15.6 us (2%)
    all_gather x1, waiting for transfers between devices, local(): lax.all_gather((jnp.dot(acts, rot_rows, preferred_element_type=jnp.float3...  197 us
    psum x2, waiting for transfers between devices, local(): lax.psum((jnp.dot(every_factor, point, preferred_element_type=jnp.float32...  170 us
    psum x1, waiting for transfers between devices, local(): lax.psum(contract_cols(grad_hidden, w_up).astype(jnp.bfloat16), MP)  88.8 us
    all_gather x1, waiting for transfers between devices, local(): rot_rows = lax.all_gather(rot_half, DP, axis=1, tiled=True)  53.8 us
    psum x4, blocking collectives, by_axis(): return functools.reduce(lax.psum, axes, value)  32.2 us
    dot_general x2, matrix products, contract_cols(): lax.dot_general(left, right, (((1,), (1,)), ((), ())), preferred_element_...  27.3 us
    all_gather x1, waiting for transfers between devices, in_one_piece(): lax.all_gather(both, axis, axis=dim, tiled=True)  26.4 us
    dot_general x2, matrix products, local(): jnp.einsum('ntr,ntc->nrc', factor_blocks, right, preferred_element_type=j...  23.1 us
  transfers between devices with their start and end apart: 6, of which 6 were waited for; matrix products, arithmetic and copies ran while one was open for 0% of the time, Pallas kernels for 0%

profile of v1, /device:TPU:1, one launch (start us, length us, event | category | flops | bytes accessed | tf_op | source)
XLA Modules:
  0.0 705.0 jit_solution(1676533232102412966)
XLA Ops:
  7.2 0.0 copy-start.7
  7.2 0.0 all-gather.5.cloned.1.call-start
  7.2 2.8 convert_element_type.66
  10.0 0.0 all-gather.5.cloned.1.call-update
  10.0 0.0 all-gather.9.cloned.1.call-start
  10.0 53.8 %all-gather.5.cloned.1.call-done = bf16[512,8192]{1,0:T(8,128)(2,1)} async-done(((bf16[512,1024]{1,0:T(8,128)(2,1)}), bf16[512,8192]{1,0:T(8,128)(2,1)}) %all-gather.5.cloned.1.call-update) | async-done | bytes 8388624 | tf_op jit(solution)/shard_map/all_gather | solution.py:44
  63.8 0.0 copy-done.7
  63.8 6.0 fusion
  69.9 0.0 all-gather.9.cloned.1.call-update
  69.9 0.0 all-reduce.10.cloned.1.call-start
  69.9 196.7 %all-gather.9.cloned.1.call-done = bf16[2048,8192]{1,0:T(8,128)(2,1)} async-done(((bf16[128,8192]{1,0:T(8,128)(2,1)}), bf16[2048,8192]{1,0:T(8,128)(2,1)}) %all-gather.9.cloned.1.call-update) | async-done | bytes 33554448 | tf_op jit(solution)/shard_map/all_gather | solution.py:46
  266.6 0.0 copy-start.8
  266.6 11.6 %reduce_sum.49 = bf16[128,8192]{1,0:T(8,128)(2,1)S(1)} reduce(bf16[16,128,8192]{2,1,0:T(8,128)(2,1)} %bitcast.24, bf16[]{:T(256)} %constant.6.clone.1), dimensions={0}, to_apply=%region_5.0 | reduce | flops 15728640 | bytes 35651584 | tf_op jit(solution)/shard_map/reduce_sum | solution.py:45
  278.2 0.0 copy-done.8
  278.3 19.6 %convolution_convert_fusion = bf16[128,8192]{1,0:T(8,128)(2,1)} fusion(bf16[8192,896]{1,0:T(8,128)(2,1)} %param.5, bf16[128,896]{1,0:T(8,128)(2,1)S(1)} %copy-done.8, bf16[128,8192]{1,0:T(8,128)(2,1)S(1)} %reduce_sum.49), kind=kOutput, calls=%fused_computation.6 | convolution fusion | flops 3760291840 | bytes 19103744 | tf_op jit(solution)/shard_map/dot_general | solution.py:36
  297.9 0.0 all-reduce.10.cloned.1.call-update
  297.9 0.0 copy-start
  297.9 0.0 all-gather.7.cloned.1.call-start
  298.0 88.8 %all-reduce.10.cloned.1.call-done = bf16[128,8192]{1,0:T(8,128)(2,1)} async-done(((bf16[128,8192]{1,0:T(8,128)(2,1)}), bf16[128,8192]{1,0:T(8,128)(2,1)}) %all-reduce.10.cloned.1.call-update) | async-done | bytes 2097168 | tf_op jit(solution)/shard_map/psum | solution.py:59
  386.8 7.7 %multiply_reduce_fusion = (f32[]{:T(128)}, bf16[128,512]{1,0:T(8,128)(2,1)S(1)}) fusion(bf16[128,8192]{1,0:T(8,128)(2,1)} %all-reduce.10.cloned.1.call-done, bf16[512,8192]{1,0:T(8,128)(2,1)} %all-gather.5.cloned.1.call-done), kind=kOutput, calls=%fused_computation.18 | convolution fusion | flops 1074003968 | bytes 10616836 | tf_op jit(solution)/shard_map/dot_general | solution.py:36
  394.4 0.7 pad_maximum_fusion
  395.1 0.0 all-gather.7.cloned.1.call-update
  395.2 0.0 all-reduce.14.cloned.1.call-start
  395.2 26.4 %all-gather.7.cloned.1.call-done = bf16[1024,1024]{1,0:T(8,128)(2,1)} async-done(((bf16[128,1024]{1,0:T(8,128)(2,1)}), bf16[1024,1024]{1,0:T(8,128)(2,1)}) %all-gather.7.cloned.1.call-update) | async-done | bytes 2097168 | tf_op jit(solution)/shard_map/all_gather | solution.py:24
  421.6 0.0 copy-done
  421.6 0.0 copy-start.5
  421.6 3.9 multiply_convert_fusion.3
  425.6 0.0 copy-done.5
  425.6 2.6 multiply_convert_fusion.2
  428.2 0.0 all-reduce.14.cloned.1.call-update
  428.2 0.0 all-reduce.12.cloned.1.call-start
  428.3 0.7 multiply_reduce_fusion.1
  428.9 7.9 %all-reduce.2 = (f32[]{:T(128)}, f32[]{:T(128)}) all-reduce(f32[]{:T(128)} %multiply_reduce_fusion.1, f32[]{:T(128)} %get-tuple-element.18), channel_id=1, replica_groups=mesh['dp_0'=4,'dp_1'=2,'mp_0'=4,'mp_1'=4] {'dp_0'}, use_global_device_ids=true, to_apply=%region_1.0 | all-reduce | flops 2 | bytes 16 | tf_op jit(solution)/shard_map/psum | solution.py:19
  436.8 5.1 all-reduce.3
  441.9 9.9 %all-reduce.1 = (f32[]{:T(128)}, f32[]{:T(128)}) all-reduce(f32[]{:T(128)} %get-tuple-element.8, f32[]{:T(128)} %get-tuple-element.9), channel_id=1, replica_groups=mesh['dp_0'=4,'dp_1'=2,'mp_0'=4,'mp_1'=4] {'mp_0'}, use_global_device_ids=true, to_apply=%region_3.0 | all-reduce | flops 2 | bytes 16 | tf_op jit(solution)/shard_map/psum | solution.py:19
  451.8 9.3 %all-reduce = (f32[]{:T(128)}, f32[]{:T(128)}) all-reduce(f32[]{:T(128)} %get-tuple-element.4, f32[]{:T(128)} %get-tuple-element.5), channel_id=1, replica_groups=mesh['dp_0'=4,'dp_1'=2,'mp_0'=4,'mp_1'=4] {'mp_1'}, use_global_device_ids=true, to_apply=%region_4.0 | all-reduce | flops 2 | bytes 16 | tf_op jit(solution)/shard_map/psum | solution.py:19
  462.6 2.6 fusion.7
  465.2 66.5 %all-reduce.14.cloned.1.call-done = (bf16[8,128,1024]{2,1,0:T(8,128)(2,1)}, bf16[8,128,1024]{2,1,0:T(8,128)(2,1)}) async-done(((bf16[8,128,1024]{2,1,0:T(8,128)(2,1)}, bf16[8,128,1024]{2,1,0:T(8,128)(2,1)}), (bf16[8,128,1024]{2,1,0:T(8,128)(2,1)}, bf16[8,128,1024]{2,1,0:T(8,128)(2,1)})) %all-reduce.14.cloned.1.call-update) | async-done | bytes 4194320 | tf_op jit(solution)/shard_map/psum | solution.py:82
  531.7 0.0 copy-start.1
  531.7 0.0 copy-start.3
  531.7 9.8 %fusion.10 = f32[8,512,1024]{2,1,0:T(8,128)} fusion(bf16[8,128,512]{2,1,0:T(8,128)(2,1)S(1)} %bitcast.25, bf16[8,128,1024]{2,1,0:T(8,128)(2,1)} %get-tuple-element.12), kind=kOutput, calls=%fused_computation.28 | convolution fusion | flops 1073741824 | bytes 19922944 | tf_op jit(solution)/shard_map/ntr,ntc->nrc/dot_general | solution.py:97
  541.6 0.0 copy-done.1
  541.6 0.0 copy-done.3
  541.6 11.4 %subtract_convert_fusion.1 = bf16[8,512,1024]{2,1,0:T(8,128)(2,1)} fusion(f32[8,512,1024]{2,1,0:T(8,128)} %fusion.10, bf16[8,128,512]{2,1,0:T(8,128)(2,1)S(1)} %bitcast.27, bf16[8,128,1024]{2,1,0:T(8,128)(2,1)S(1)} %copy-done.3), kind=kOutput, calls=%fused_computation.3 | convolution fusion | flops 1082130432 | bytes 28311552 | tf_op jit(solution)/shard_map/ntr,ntc->nrc/dot_general | solution.py:99
  553.0 5.7 convert_reduce_fusion.1
  558.7 0.0 copy-start.6
  558.7 1.8 add_convert_fusion
  560.5 0.0 copy-done.6
  560.5 2.6 multiply_convert_fusion
  563.1 2.6 multiply_convert_fusion.1
  565.7 0.0 all-reduce.12.cloned.1.call-update
  565.8 103.4 %all-reduce.12.cloned.1.call-done = (bf16[8,128,1024]{2,1,0:T(8,128)(2,1)}, bf16[8,128,1024]{2,1,0:T(8,128)(2,1)}) async-done(((bf16[8,128,1024]{2,1,0:T(8,128)(2,1)}, bf16[8,128,1024]{2,1,0:T(8,128)(2,1)}), (bf16[8,128,1024]{2,1,0:T(8,128)(2,1)}, bf16[8,128,1024]{2,1,0:T(8,128)(2,1)})) %all-reduce.12.cloned.1.call-update) | async-done | bytes 4194320 | tf_op jit(solution)/shard_map/psum | solution.py:82
  669.2 0.0 copy-start.2
  669.2 0.0 copy-start.4
  669.2 9.8 %fusion.11 = f32[8,512,1024]{2,1,0:T(8,128)} fusion(bf16[8,128,512]{2,1,0:T(8,128)(2,1)S(1)} %bitcast.26, bf16[8,128,1024]{2,1,0:T(8,128)(2,1)} %get-tuple-element.10), kind=kOutput, calls=%fused_computation.29 | convolution fusion | flops 1073741824 | bytes 19922944 | tf_op jit(solution)/shard_map/ntr,ntc->nrc/dot_general | solution.py:97
  679.0 0.0 copy-done.2
  679.0 0.0 copy-done.4
  679.0 11.7 %subtract_convert_fusion = bf16[8,512,1024]{2,1,0:T(8,128)(2,1)} fusion(f32[8,512,1024]{2,1,0:T(8,128)} %fusion.11, bf16[8,128,512]{2,1,0:T(8,128)(2,1)S(1)} %bitcast.28, bf16[8,128,1024]{2,1,0:T(8,128)(2,1)S(1)} %copy-done.4), kind=kOutput, calls=%fused_computation.1 | convolution fusion | flops 1082130432 | bytes 28311552 | tf_op jit(solution)/shard_map/ntr,ntc->nrc/dot_general | solution.py:99
  690.7 5.7 convert_reduce_fusion
  696.4 1.8 multiply_subtract_fusion
Async XLA Ops:
  7.2 56.7 %copy-start.7 = (bf16[128,512]{1,0:T(8,128)(2,1)S(1)}, bf16[128,512]{1,0:T(8,128)(2,1)}, u32[]{:S(2)}) copy-start(bf16[128,512]{1,0:T(8,128)(2,1)} %param.4) | copy-start | bytes 393220
  7.2 56.7 %all-gather.5.cloned.1.call-start = ((), (), s32[]{:S(2)}) async-start(), calls=%async_computation | async-start | bytes 9437184 | tf_op jit(solution)/shard_map/all_gather | solution.py:44
  10.0 256.6 %all-gather.9.cloned.1.call-start = ((), (), s32[]{:S(2)}) async-start(), calls=%async_computation.3 | async-start | bytes 35651584 | tf_op jit(solution)/shard_map/all_gather | solution.py:46
  69.9 316.9 %all-reduce.10.cloned.1.call-start = ((), (), s32[]{:S(2)}) async-start(), calls=%async_computation.1 | async-start | bytes 4194304 | tf_op jit(solution)/shard_map/psum | solution.py:59
  266.6 11.6 %copy-start.8 = (bf16[128,896]{1,0:T(8,128)(2,1)S(1)}, bf16[128,896]{1,0:T(8,128)(2,1)}, u32[]{:S(2)}) copy-start(bf16[128,896]{1,0:T(8,128)(2,1)} %param.6) | copy-start | bytes 688132
  297.9 123.7 %copy-start = (f32[512,1024]{1,0:T(8,128)S(1)}, f32[512,1024]{1,0:T(8,128)}, u32[]{:S(2)}) copy-start(f32[512,1024]{1,0:T(8,128)} %param.7) | copy-start | bytes 6291460
  297.9 123.7 %all-gather.7.cloned.1.call-start = ((), (), s32[]{:S(2)}) async-start(), calls=%async_computation.2 | async-start | bytes 2359296 | tf_op jit(solution)/shard_map/all_gather | solution.py:24
  395.2 136.6 %all-reduce.14.cloned.1.call-start = ((), (), s32[]{:S(2)}) async-start(), calls=%async_computation.5 | async-start | bytes 8388608 | tf_op jit(solution)/shard_map/psum | solution.py:82
  421.6 4.0 copy-start.5
  428.2 241.0 %all-reduce.12.cloned.1.call-start = ((), (), s32[]{:S(2)}) async-start(), calls=%async_computation.4 | async-start | bytes 8388608 | tf_op jit(solution)/shard_map/psum | solution.py:82
  531.7 9.8 %copy-start.1 = (bf16[1024,512]{1,0:T(8,128)(2,1)S(1)}, bf16[1024,512]{1,0:T(8,128)(2,1)}, u32[]{:S(2)}) copy-start(bf16[1024,512]{1,0:T(8,128)(2,1)} %get-tuple-element.16) | copy-start | bytes 3145732
  531.7 9.8 %copy-start.3 = (bf16[8,128,1024]{2,1,0:T(8,128)(2,1)S(1)}, bf16[8,128,1024]{2,1,0:T(8,128)(2,1)}, u32[]{:S(2)}) copy-start(bf16[8,128,1024]{2,1,0:T(8,128)(2,1)} %get-tuple-element.13) | copy-start | bytes 6291460
  558.7 1.9 copy-start.6
  669.2 9.8 %copy-start.2 = (bf16[1024,512]{1,0:T(8,128)(2,1)S(1)}, bf16[1024,512]{1,0:T(8,128)(2,1)}, u32[]{:S(2)}) copy-start(bf16[1024,512]{1,0:T(8,128)(2,1)} %get-tuple-element.16) | copy-start | bytes 3145732
  669.2 9.8 %copy-start.4 = (bf16[8,128,1024]{2,1,0:T(8,128)(2,1)S(1)}, bf16[8,128,1024]{2,1,0:T(8,128)(2,1)}, u32[]{:S(2)}) copy-start(bf16[8,128,1024]{2,1,0:T(8,128)(2,1)} %get-tuple-element.11) | copy-start | bytes 6291460
Sparse Core Ops, SparseCore 0:
  10.3 53.5 all-gather.4
  70.0 196.5 all-gather.8
  298.0 88.6 all-reduce.9
  395.3 26.2 all-gather.6
  428.3 103.3 all-reduce.13
  565.9 103.2 all-reduce.11
